TPU v7x, 32 devices: a whole 2x2x4 slice. The times are simulated.
32 devices in a mesh: grp: 2 (over x), wide: 16 (over z, y, core).
Axes of the slice: x: 2, y: 2, z: 4, core: 2. Of those that a mesh axis runs over, the one named last changes fastest.
Arguments:
- raw: bfloat16 [4096, 16, 2048], P(('grp', 'wide')), parts along dimension 0, may hold values from -6 to 6
- cell_feed: int32 [1024], replicated, may hold values from 0 to 1023, each once
- dm_delay: int32 [1024, 1024], replicated, may hold values from 0 to 15
Outputs:
- dedispersed: float32 [2048, 16, 1024], P(('grp', 'wide')), parts along dimension 0
There are 2 independent parts, one for each index of `grp`. A program takes and returns all parts, laid end to end along the dimension named above; an argument that names none is the same for every part. Nothing has to cross between parts.
Inputs may be any that keep to these rules, and one draw needn't show every extreme that they name: `cell_feed`: every antenna stands at exactly one cell.
All inputs are finite; a program needn't handle non-finite values.
Results may differ from a plain program's by a relative error of at most 0.0084.
Values may be sent and summed in bfloat16 or wider, within the bound.
No kernel may reach another device: no remote copies, remote signals or barrier semaphores. Data moves between devices by JAX's collectives and lax.ppermute only.
A program may use at most 128 MiB of HBM per device.

v0:
```python
import math
import jax
import jax.numpy as jnp
import numpy as np
from jax import lax
from jax.sharding import PartitionSpec as P

EAST_COSINE = np.array([[1, 1, 1, 1], [1, 0, -1, 0], [1, -1, 1, -1], [1, 0, -1, 0]], np.float32)
EAST_SINE = np.array([[0, 0, 0, 0], [0, 1, 0, -1], [0, 0, 0, 0], [0, -1, 0, 1]], np.float32)


def phase_pair(count, length):
    angle = (count % length).astype(jnp.float32) * (2.0 * math.pi / length)
    return (jnp.cos(angle), jnp.sin(angle))


def channel_table(samples, width):
    sample_ids = lax.broadcasted_iota(jnp.int32, (samples, width), 0)
    freq_ids = lax.broadcasted_iota(jnp.int32, (samples, width), 1)
    cosine, sine = phase_pair(sample_ids * freq_ids, samples)
    factor = 1.0 / math.sqrt(samples)
    return jnp.concatenate([cosine * factor, -sine * factor], axis=1).astype(jnp.bfloat16)


def sky_table(cells):
    rows = lax.broadcasted_iota(jnp.int32, (cells, cells), 0)
    cols = lax.broadcasted_iota(jnp.int32, (cells, cells), 1)
    cosine, sine = phase_pair(rows * cols, cells)
    real_row = jnp.stack([cosine, sine], axis=-1)
    imag_row = jnp.stack([-sine, cosine], axis=-1)
    factor = 1.0 / math.sqrt(cells)
    return (jnp.stack([real_row, imag_row], axis=1) * factor).astype(jnp.bfloat16)


def transform_table(frames):
    terms = frames // 2 + 1
    harmonic = lax.broadcasted_iota(jnp.int32, (terms, frames), 0)
    moment = lax.broadcasted_iota(jnp.int32, (terms, frames), 1)
    cosine, sine = phase_pair(harmonic * moment, frames)
    return jnp.stack([cosine, -sine]).astype(jnp.bfloat16)


def beam_power(spec, feed_index, table):
    grid = jnp.take(spec, feed_index.reshape(-1), axis=0)
    grid = grid.reshape(feed_index.shape + spec.shape[1:])
    beams = jnp.einsum("joni,penrif->poerfj", table, grid, preferred_element_type=jnp.float32)
    real_part = beams[:, 0]
    imag_part = beams[:, 1]
    cosines = jnp.asarray(EAST_COSINE)
    sines = jnp.asarray(EAST_SINE)
    high = lax.Precision.HIGHEST
    east_real = 0.5 * (
        jnp.einsum("qe,perfj->prfqj", cosines, real_part, precision=high)
        + jnp.einsum("qe,perfj->prfqj", sines, imag_part, precision=high)
    )
    east_imag = 0.5 * (
        jnp.einsum("qe,perfj->prfqj", cosines, imag_part, precision=high)
        - jnp.einsum("qe,perfj->prfqj", sines, real_part, precision=high)
    )
    power = 0.5 * jnp.sum(east_real * east_real + east_imag * east_imag, axis=0)
    return power.reshape(power.shape[0], power.shape[1], -1)


def dedisperse(spectrum, dm_delay, frames):
    base_cos, base_sin = phase_pair(jnp.transpose(dm_delay), frames)
    beams_dev = spectrum.shape[3]
    nfreq = spectrum.shape[2]

    def one_term(carry, block):
        cosine, sine = carry
        cos_half = cosine.astype(jnp.bfloat16)
        sin_half = sine.astype(jnp.bfloat16)
        upper = jnp.concatenate([cos_half, sin_half], axis=1)
        lower = jnp.concatenate([-sin_half, cos_half], axis=1)
        right = jnp.concatenate([upper, lower], axis=0)
        left = block.reshape(2 * nfreq, beams_dev)
        result = lax.dot_general(
            left, right, (((0,), (0,)), ((), ())), preferred_element_type=jnp.float32
        )
        next_cos = cosine * base_cos - sine * base_sin
        next_sin = sine * base_cos + cosine * base_sin
        return ((next_cos, next_sin), result)

    start = (jnp.ones(base_cos.shape, jnp.float32), jnp.zeros(base_cos.shape, jnp.float32))
    final, trials = lax.scan(one_term, start, spectrum)
    return trials.reshape(trials.shape[0], beams_dev, 2, -1)


def synthesis(trials, frames, nfreq):
    terms = frames // 2 + 1
    moment = lax.broadcasted_iota(jnp.int32, (frames, terms), 0)
    harmonic = lax.broadcasted_iota(jnp.int32, (frames, terms), 1)
    cosine, sine = phase_pair(moment * harmonic, frames)
    weight = jnp.where((harmonic == 0) | (harmonic * 2 == frames), 1.0, 2.0).astype(jnp.float32)
    weight = weight / (frames * math.sqrt(nfreq))
    table = jnp.stack([cosine * weight, -sine * weight], axis=1)
    return jnp.einsum("tuk,kbud->btd", table, trials, precision=lax.Precision.HIGHEST)


def body(raw, cell_feed, dm_delay):
    feed_dev, frames, samples = raw.shape
    nfreq = samples // 2
    table = channel_table(samples, nfreq)
    spectra = jnp.dot(
        raw.reshape(feed_dev * frames, samples), table, preferred_element_type=jnp.float32
    )
    spectra = spectra.astype(jnp.bfloat16).reshape(feed_dev, frames, 2, nfreq)
    cells = cell_feed.shape[0] // 4
    polar = lax.broadcasted_iota(jnp.int32, (2, 4, cells), 0)
    feed_index = 2 * cell_feed.reshape(1, 4, cells) + polar
    table_sky = sky_table(cells)
    arrived = lax.all_to_all(spectra, "wide", split_axis=3, concat_axis=0, tiled=True)
    power = beam_power(arrived, feed_index, table_sky)
    centred = (power - jnp.mean(power, axis=0, keepdims=True)).astype(jnp.bfloat16)
    time_table = transform_table(frames)
    local = jnp.einsum("okr,rfb->kofb", time_table, centred, preferred_element_type=jnp.float32)
    spectrum = lax.all_to_all(
        local.astype(jnp.bfloat16), "wide", split_axis=3, concat_axis=2, tiled=True
    )
    trials = dedisperse(spectrum, dm_delay, frames)
    return synthesis(trials, frames, nfreq)


def solution(mesh):
    placed = (P(("grp", "wide"), None, None), P(), P())
    return jax.shard_map(
        body, mesh=mesh, in_specs=placed, out_specs=P(("grp", "wide"), None, None), check_vma=False
    )
```

profile of v0, /device:TPU:13, one launch (start us, length us, event | category | flops | bytes accessed | tf_op | source)
XLA Modules:
  0.0 774.5 jit_solution(11408778004443474924)
XLA Ops:
  0.0 34.1 %multiply_convert_fusion = (bf16[2048,1024]{1,0:T(8,128)(2,1)S(1)}, bf16[2048,1024]{1,0:T(8,128)(2,1)S(1)}) fusion(), kind=kLoop, calls=%fused_computation.36 | loop fusion | flops 39845888 | bytes 8388608 | tf_op jit(solution)/shard_map/convert.3
  34.1 20.6 %convert_bitcast_fusion = bf16[2048,2048]{0,1:T(8,128)(2,1)} fusion(bf16[2048,2048]{1,0:T(8,128)(2,1)S(1)} %bitcast.101, bf16[2048,1024]{1,0:T(8,128)(2,1)S(1)} %get-tuple-element.115, bf16[2048,1024]{1,0:T(8,128)(2,1)S(1)} %get-tuple-element.116), kind=kOutput, calls=%fused_computation.35 | convolution fusion | flops 17200840704 | bytes 25165824 | tf_op jit(solution)/shard_map/dot_general | solution.py:104
  54.7 12.4 %copy.57 = bf16[2048,2048]{1,0:T(8,128)(2,1)} copy(bf16[2048,2048]{0,1:T(8,128)(2,1)} %convert_bitcast_fusion) | data formatting | bytes 16777216 | tf_op jit(solution)/shard_map/convert_element_type | solution.py:107
  67.1 14.5 %reshape.314 = bf16[128,16,2,1024]{3,2,1,0:T(2,128)(2,1)} reshape(bf16[2048,2048]{1,0:T(8,128)(2,1)} %copy.57) | data formatting | bytes 16777216 | tf_op jit(solution)/shard_map/reshape | solution.py:107
  81.6 16.8 %copy.58 = bf16[128,16,2,1024]{0,1,2,3:T(8,128)(2,1)} copy(bf16[128,16,2,1024]{3,2,1,0:T(2,128)(2,1)} %reshape.314) | data formatting | bytes 16777216 | tf_op jit(solution)/shard_map/reshape | solution.py:107
  107.7 179.9 %all-to-all-done = bf16[128,16,2,1024]{0,1,2,3:T(8,128)(2,1)} async-done(((bf16[128,16,2,1024]{0,1,2,3:T(8,128)(2,1)}), bf16[128,16,2,1024]{0,1,2,3:T(8,128)(2,1)}, u32[]{:S(2)}, u32[]{:S(2)}) %all-to-all-start) | async-done | bytes 8388640 | tf_op jit(solution)/shard_map/all_to_all | solution.py:112
  287.6 29.0 %copy.82 = bf16[16,128,16,2,64]{4,2,3,1,0:T(8,128)(2,1)} copy(bf16[16,128,16,2,64]{1,2,3,4,0:T(8,128)(2,1)} %bitcast.5) | data formatting | bytes 16777216 | tf_op jit(solution)/shard_map/all_to_all | solution.py:112
  316.7 25.0 %gather_fusion = bf16[2048,16,2,64]{3,1,2,0:T(8,128)(2,1)} fusion(bf16[2048,16,2,64]{3,1,2,0:T(8,128)(2,1)} %bitcast.92, s32[2048]{0:T(1024)S(1)} %broadcast_clamp_fusion), kind=kCustom, calls=%fused_computation | custom fusion | bytes 16785408 | tf_op jit(solution)/shard_map/jit(_take)/gather | solution.py:44
  341.7 19.8 %copy.83 = bf16[2,4,256,16,2,64]{2,1,0,5,4,3:T(4,128)(2,1)} copy(bf16[2,4,256,16,2,64]{5,3,4,2,1,0:T(8,128)(2,1)} %bitcast.93) | data formatting | bytes 16777216 | tf_op jit(solution)/shard_map/jit(_take)/gather | solution.py:44
  367.2 8.2 %fusion.39 = f32[2,2,4,16,64,256]{5,4,1,3,2,0:T(8,128)} fusion(bf16[2,4,256,16,2,64,1]{2,1,0,5,4,3,6:T(4,128)(2,1)S(1)} %select_bitcast_fusion, f32[256,1,256,2]{2,0,3,1:T(8,128)S(1)} %get-tuple-element.112, f32[256,1,256,2]{2,0,3,1:T(8,128)S(1)} %get-tuple-element.111), kind=kOutput, calls=%fused_computation.49 | convolution fusion | flops 4295753728 | bytes 26214400 | tf_op jit(solution)/shard_map/joni,penrif->poerfj/dot_general | solution.py:46
  382.0 18.8 %fusion.31 = f32[2,16,64,256,4]{3,4,2,1,0:T(4,128)} fusion(f32[4,4,1,1,1]{1,0,4,3,2:T(4,128)S(1)} %copy-done.3, f32[2,4,16,64,256]{4,3,2,1,0:T(8,128)S(1)} %get-tuple-element.108), kind=kOutput, calls=%fused_computation.41 | convolution fusion | flops 100663296 | bytes 16777280 | tf_op jit(solution)/shard_map/qe,perfj->prfqj/dot_general | solution.py:57
  400.8 18.4 %fusion.33 = f32[2,16,64,256,4]{3,4,2,1,0:T(4,128)} fusion(f32[4,4,1,1,1]{1,0,4,3,2:T(4,128)S(1)} %copy-done.4, f32[2,4,16,64,256]{4,3,2,1,0:T(8,128)S(1)} %get-tuple-element.108), kind=kOutput, calls=%fused_computation.43 | convolution fusion | flops 100663296 | bytes 16777280 | tf_op jit(solution)/shard_map/qe,perfj->prfqj/dot_general | solution.py:54
  419.2 18.5 %fusion.35 = f32[2,16,64,256,4]{3,4,2,1,0:T(4,128)} fusion(f32[4,4,1,1,1]{1,0,4,3,2:T(4,128)S(1)} %copy-done.4, f32[2,4,16,64,256]{4,3,2,1,0:T(8,128)S(1)} %get-tuple-element.107), kind=kOutput, calls=%fused_computation.45 | convolution fusion | flops 100663296 | bytes 16777280 | tf_op jit(solution)/shard_map/qe,perfj->prfqj/dot_general | solution.py:58
  437.7 32.8 %add_reduce_fusion = f32[16,64,256,4]{2,3,1,0:T(4,128)} fusion(f32[2,16,64,256,4]{3,4,2,1,0:T(4,128)} %fusion.31, f32[2,16,64,256,4]{3,4,2,1,0:T(4,128)} %fusion.35, f32[2,16,64,256,4]{3,4,2,1,0:T(4,128)} %fusion.33, f32[4,4,1,1,1]{1,0,4,3,2:T(4,128)S(1)} %copy-done.3, f32[2,4,16,64,256]{4,3,2,1,0:T(8,128)} %copy-done.1), kind=kOutput, calls=%fused_computation.33 | convolution fusion | flops 116391936 | bytes 37748800 | tf_op jit(solution)/shard_map/qe,perfj->prfqj/dot_general | solution.py:53
  482.8 7.1 convert_bitcast_fusion.1
  489.9 14.7 %copy.69 = bf16[9,2,64,1024]{2,1,0,3:T(2,128)(2,1)} copy(bf16[9,2,64,1024]{3,0,1,2:T(8,128)(2,1)} %convert_bitcast_fusion.1) | data formatting | bytes 4718592 | tf_op jit(solution)/shard_map/convert_element_type | solution.py:118
  504.6 7.8 %reshape.334 = bf16[16,2,36864]{2,1,0:T(2,128)(2,1)} reshape(bf16[1024,9,2,64]{3,2,1,0:T(2,128)(2,1)} %bitcast.94) | data formatting | bytes 4718592
  523.0 18.4 %fusion.55 = (f32[1024,1024]{1,0:T(8,128)}, f32[1024,1024]{1,0:T(8,128)}) fusion(s32[1024,1024]{0,1:T(8,128)} %copy.56), kind=kLoop, calls=%fused_computation.65 | loop fusion | flops 13631488 | bytes 12582912 | tf_op jit(solution)/shard_map/sin | solution.py:14
  541.4 29.1 %all-to-all-done.1 = bf16[16,2,36864]{2,1,0:T(2,128)(2,1)S(1)} async-done(((bf16[16,2,36864]{2,1,0:T(2,128)(2,1)}), bf16[16,2,36864]{2,1,0:T(2,128)(2,1)S(1)}, u32[]{:S(2)}, u32[]{:S(2)}) %all-to-all-start.1) | async-done | bytes 2359328 | tf_op jit(solution)/shard_map/all_to_all | solution.py:117
  575.8 11.5 %copy.90 = bf16[9,2,64,16,64]{4,2,3,1,0:T(8,128)(2,1)} copy(bf16[9,2,64,16,64]{2,1,0,4,3:T(2,128)(2,1)} %bitcast.95) | data formatting | bytes 4718592 | tf_op jit(solution)/shard_map/all_to_all | solution.py:117
  587.2 166.2 %while.15 = (s32[]{:T(128)}, f32[1024,1024]{1,0:T(8,128)}, f32[1024,1024]{1,0:T(8,128)}, f32[9,64,2048]{2,1,0:T(8,128)}, f32[1024,1024]{1,0:T(8,128)}, /*index=5...) while((s32[]{:T(128)}, f32[1024,1024]{1,0:T(8,128)}, ...), condition=%wide.region_3.4_spmd.clone, body=%wide.region_2.3_spmd.clone.sunk | while | flops 584056832 | bytes 64225924 | solution.py:85
  592.3 8.2 %multiply_add_fusion.2 = (f32[1024,1024]{1,0:T(8,128)}, f32[1024,1024]{1,0:T(8,128)}) fusion(f32[1024,1024]{1,0:T(8,128)S(1)} %copy-done, f32[1024,1024]{1,0:T(8,128)} %get-tuple-element.196, f32[1024,1024]{1,0:T(8,128)} %get-tuple-element.185, f32[1024,1024]{1,0:T(8,128)} %get-tuple-element.184, pred[]{:T(512)S(6)} %compare.38), kind=kLoop, calls=%fused_computation.9.clone.1 | loop fusion | flops 8388608 | bytes 25165824 | tf_op jit(solution)/shard_map/while/body/eval_jaxpr/add | solution.py:81
  608.9 10.6 %multiply_add_fusion.2 = (f32[1024,1024]{1,0:T(8,128)}, f32[1024,1024]{1,0:T(8,128)}) fusion(f32[1024,1024]{1,0:T(8,128)S(1)} %copy-done, f32[1024,1024]{1,0:T(8,128)} %get-tuple-element.196, f32[1024,1024]{1,0:T(8,128)} %get-tuple-element.185, f32[1024,1024]{1,0:T(8,128)} %get-tuple-element.184, pred[]{:T(512)S(6)} %compare.38), kind=kLoop, calls=%fused_computation.9.clone.1 | loop fusion | flops 8388608 | bytes 25165824 | tf_op jit(solution)/shard_map/while/body/eval_jaxpr/add | solution.py:81
  628.1 10.6 %multiply_add_fusion.2 = (f32[1024,1024]{1,0:T(8,128)}, f32[1024,1024]{1,0:T(8,128)}) fusion(f32[1024,1024]{1,0:T(8,128)S(1)} %copy-done, f32[1024,1024]{1,0:T(8,128)} %get-tuple-element.196, f32[1024,1024]{1,0:T(8,128)} %get-tuple-element.185, f32[1024,1024]{1,0:T(8,128)} %get-tuple-element.184, pred[]{:T(512)S(6)} %compare.38), kind=kLoop, calls=%fused_computation.9.clone.1 | loop fusion | flops 8388608 | bytes 25165824 | tf_op jit(solution)/shard_map/while/body/eval_jaxpr/add | solution.py:81
  647.2 10.6 %multiply_add_fusion.2 = (f32[1024,1024]{1,0:T(8,128)}, f32[1024,1024]{1,0:T(8,128)}) fusion(f32[1024,1024]{1,0:T(8,128)S(1)} %copy-done, f32[1024,1024]{1,0:T(8,128)} %get-tuple-element.196, f32[1024,1024]{1,0:T(8,128)} %get-tuple-element.185, f32[1024,1024]{1,0:T(8,128)} %get-tuple-element.184, pred[]{:T(512)S(6)} %compare.38), kind=kLoop, calls=%fused_computation.9.clone.1 | loop fusion | flops 8388608 | bytes 25165824 | tf_op jit(solution)/shard_map/while/body/eval_jaxpr/add | solution.py:81
  666.3 10.6 %multiply_add_fusion.2 = (f32[1024,1024]{1,0:T(8,128)}, f32[1024,1024]{1,0:T(8,128)}) fusion(f32[1024,1024]{1,0:T(8,128)S(1)} %copy-done, f32[1024,1024]{1,0:T(8,128)} %get-tuple-element.196, f32[1024,1024]{1,0:T(8,128)} %get-tuple-element.185, f32[1024,1024]{1,0:T(8,128)} %get-tuple-element.184, pred[]{:T(512)S(6)} %compare.38), kind=kLoop, calls=%fused_computation.9.clone.1 | loop fusion | flops 8388608 | bytes 25165824 | tf_op jit(solution)/shard_map/while/body/eval_jaxpr/add | solution.py:81
  685.4 10.6 %multiply_add_fusion.2 = (f32[1024,1024]{1,0:T(8,128)}, f32[1024,1024]{1,0:T(8,128)}) fusion(f32[1024,1024]{1,0:T(8,128)S(1)} %copy-done, f32[1024,1024]{1,0:T(8,128)} %get-tuple-element.196, f32[1024,1024]{1,0:T(8,128)} %get-tuple-element.185, f32[1024,1024]{1,0:T(8,128)} %get-tuple-element.184, pred[]{:T(512)S(6)} %compare.38), kind=kLoop, calls=%fused_computation.9.clone.1 | loop fusion | flops 8388608 | bytes 25165824 | tf_op jit(solution)/shard_map/while/body/eval_jaxpr/add | solution.py:81
  704.5 10.6 %multiply_add_fusion.2 = (f32[1024,1024]{1,0:T(8,128)}, f32[1024,1024]{1,0:T(8,128)}) fusion(f32[1024,1024]{1,0:T(8,128)S(1)} %copy-done, f32[1024,1024]{1,0:T(8,128)} %get-tuple-element.196, f32[1024,1024]{1,0:T(8,128)} %get-tuple-element.185, f32[1024,1024]{1,0:T(8,128)} %get-tuple-element.184, pred[]{:T(512)S(6)} %compare.38), kind=kLoop, calls=%fused_computation.9.clone.1 | loop fusion | flops 8388608 | bytes 25165824 | tf_op jit(solution)/shard_map/while/body/eval_jaxpr/add | solution.py:81
  723.7 10.6 %multiply_add_fusion.2 = (f32[1024,1024]{1,0:T(8,128)}, f32[1024,1024]{1,0:T(8,128)}) fusion(f32[1024,1024]{1,0:T(8,128)S(1)} %copy-done, f32[1024,1024]{1,0:T(8,128)} %get-tuple-element.196, f32[1024,1024]{1,0:T(8,128)} %get-tuple-element.185, f32[1024,1024]{1,0:T(8,128)} %get-tuple-element.184, pred[]{:T(512)S(6)} %compare.38), kind=kLoop, calls=%fused_computation.9.clone.1 | loop fusion | flops 8388608 | bytes 25165824 | tf_op jit(solution)/shard_map/while/body/eval_jaxpr/add | solution.py:81
  742.8 10.6 %multiply_add_fusion.2 = (f32[1024,1024]{1,0:T(8,128)}, f32[1024,1024]{1,0:T(8,128)}) fusion(f32[1024,1024]{1,0:T(8,128)S(1)} %copy-done, f32[1024,1024]{1,0:T(8,128)} %get-tuple-element.196, f32[1024,1024]{1,0:T(8,128)} %get-tuple-element.185, f32[1024,1024]{1,0:T(8,128)} %get-tuple-element.184, pred[]{:T(512)S(6)} %compare.38), kind=kLoop, calls=%fused_computation.9.clone.1 | loop fusion | flops 8388608 | bytes 25165824 | tf_op jit(solution)/shard_map/while/body/eval_jaxpr/add | solution.py:81
  753.5 7.4 reshape.315
  760.8 13.1 %fusion.48 = f32[64,16,1024]{2,1,0:T(8,128)} fusion(f32[9,64,2,1024]{3,2,1,0:T(2,128)} %reshape.315, f32[16,1,9]{2,0,1:T(8,128)S(1)} %get-tuple-element.114, f32[16,1,9]{2,0,1:T(8,128)S(1)} %get-tuple-element.113), kind=kOutput, calls=%fused_computation.60 | convolution fusion | flops 226492704 | bytes 8914048 | tf_op jit(solution)/shard_map/tuk,kbud->btd/dot_general | solution.py:97
  (84 shorter events, 122.3 us)
Async XLA Ops:
  0.0 34.1 %copy-start.6 = (bf16[128,16,2048]{2,1,0:T(8,128)(2,1)S(1)}, bf16[128,16,2048]{2,1,0:T(8,128)(2,1)}, u32[]{:S(2)}) copy-start(bf16[128,16,2048]{2,1,0:T(8,128)(2,1)} %param.7) | copy-start | bytes 25165828
  98.4 7.0 copy-start.5
  98.4 189.2 %all-to-all-start = ((bf16[128,16,2,1024]{0,1,2,3:T(8,128)(2,1)}), bf16[128,16,2,1024]{0,1,2,3:T(8,128)(2,1)}, u32[]{:S(2)}, u32[]{:S(2)}) async-start(bf16[128,16,2,1024]{0,1,2,3:T(8,128)(2,1)} %copy.58), calls=%async_computation | async-start | bytes 16777216 | tf_op jit(solution)/shard_map/all_to_all | solution.py:112
  375.4 6.5 copy-start.3
  381.9 37.2 %copy-start.1 = (f32[2,4,16,64,256]{4,3,2,1,0:T(8,128)}, f32[2,4,16,64,256]{4,3,2,1,0:T(8,128)S(1)}, u32[]{:S(2)}) copy-start(f32[2,4,16,64,256]{4,3,2,1,0:T(8,128)S(1)} %get-tuple-element.107) | copy-start | bytes 25165828
  382.0 18.8 %copy-start.4 = (f32[4,4,1,1,1]{1,0,4,3,2:T(4,128)S(1)}, f32[4,4,1,1,1]{1,0,4,3,2:T(4,128)}, u32[]{:S(2)}) copy-start(f32[4,4,1,1,1]{1,0,4,3,2:T(4,128)} %constant.123) | copy-start | bytes 196
  470.5 5.4 copy-start.2
  512.5 58.0 %all-to-all-start.1 = ((bf16[16,2,36864]{2,1,0:T(2,128)(2,1)}), bf16[16,2,36864]{2,1,0:T(2,128)(2,1)S(1)}, u32[]{:S(2)}, u32[]{:S(2)}) async-start(bf16[16,2,36864]{2,1,0:T(2,128)(2,1)} %reshape.334), calls=%async_computation.1 | async-start | bytes 4718592 | tf_op jit(solution)/shard_map/all_to_all | solution.py:117
  589.8 2.4 copy-start
  606.5 2.5 copy-start
  625.6 2.4 copy-start
  644.7 2.4 copy-start
  663.8 2.4 copy-start
  682.9 2.4 copy-start
  702.1 2.5 copy-start
  721.2 2.5 copy-start
  740.4 2.5 copy-start
where the time goes:
time: 784 us; the launch traced here: 774 us
  waiting for transfers between devices  209 us (27%)
  other arithmetic  201 us (26%)
  local copies, waits for them, and re-layouts  192 us (24%)
  matrix products  160 us (20%)
  starting transfers between devices  12.1 us (2%)
    all_to_all x1, waiting for transfers between devices, body(): lax.all_to_all(spectra, 'wide', split_axis=3, concat_axis=0, tiled=True)  180 us
    add x9, other arithmetic, one_term(): next_sin = sine * base_cos + cosine * base_sin  93.3 us
    gather x2, local copies, waits for them, and re-layouts, beam_power(): grid = jnp.take(spec, feed_index.reshape(-1), axis=0)  44.8 us
    neg x9, other arithmetic, one_term(): lower = jnp.concatenate([-sin_half, cos_half], axis=1)  41 us
    another operation x2, other arithmetic  34.1 us
    dot_general x1, matrix products, beam_power(): jnp.einsum('qe,perfj->prfqj', cosines, real_part, precision=high)  32.8 us
    reshape x2, local copies, waits for them, and re-layouts, body(): spectra = spectra.astype(jnp.bfloat16).reshape(feed_dev, frames, 2, nfreq)  31.3 us
    all_to_all x1, waiting for transfers between devices, body(): lax.all_to_all(local.astype(jnp.bfloat16), 'wide', split_axis=3, concat_a...  29.1 us
  transfers between devices with their start and end apart: 2, of which 2 were waited for; matrix products, arithmetic and copies ran while one was open for 3% of the time, Pallas kernels for 0%

commit v1 on v0

--- a/solution.py
+++ b/solution.py
@@ -4,9 +4,16 @@
 import numpy as np
 from jax import lax
 from jax.sharding import PartitionSpec as P
+from jax.lax import all_to_all, axis_size
 
 EAST_COSINE = np.array([[1, 1, 1, 1], [1, 0, -1, 0], [1, -1, 1, -1], [1, 0, -1, 0]], np.float32)
 EAST_SINE = np.array([[0, 0, 0, 0], [0, 1, 0, -1], [0, 0, 0, 0], [0, -1, 0, 1]], np.float32)
+update_ladders_for = lambda field_in, dimension_no, axis_k: jnp.concatenate(
+    all_to_all(
+        jnp.stack(jnp.split(field_in, axis_size("wide"), axis=dimension_no), axis=0), "wide", 0, 0
+    ),
+    axis=axis_k,
+)
 
 
 def phase_pair(count, length):
@@ -114,9 +121,7 @@
     centred = (power - jnp.mean(power, axis=0, keepdims=True)).astype(jnp.bfloat16)
     time_table = transform_table(frames)
     local = jnp.einsum("okr,rfb->kofb", time_table, centred, preferred_element_type=jnp.float32)
-    spectrum = lax.all_to_all(
-        local.astype(jnp.bfloat16), "wide", split_axis=3, concat_axis=2, tiled=True
-    )
+    spectrum = update_ladders_for(local.astype(jnp.bfloat16), 3, 2)
     trials = dedisperse(spectrum, dm_delay, frames)
     return synthesis(trials, frames, nfreq)
 

time: 784 us -> 770 us (0.982)
  local copies, waits for them, and re-layouts: 192 us -> 180 us
    convert_element_type x1 -> x0, local copies, waits for them, and re-layouts: 14.7 us -> none  [body(): local.astype(jnp.bfloat16)]
    all_to_all x1 -> x0, local copies, waits for them, and re-layouts: 11.5 us -> none  [body(): lax.all_to_all(local.astype(jnp.bfloat16), 'wide', split_axis=3, concat_a...]
    unnamed x16 -> x32, local copies, waits for them, and re-layouts: 18.5 us -> 28.2 us
where the time goes in v1:
time: 770 us; the launch traced here: 761 us
  waiting for transfers between devices  209 us (27%)
  other arithmetic  201 us (26%)
  local copies, waits for them, and re-layouts  180 us (23%)
  matrix products  158 us (21%)
  starting transfers between devices  12.3 us (2%)
    all_to_all x1, waiting for transfers between devices, body(): lax.all_to_all(spectra, 'wide', split_axis=3, concat_axis=0, tiled=True)  180 us
    add x9, other arithmetic, one_term(): next_sin = sine * base_cos + cosine * base_sin  93.3 us
    gather x2, local copies, waits for them, and re-layouts, beam_power(): grid = jnp.take(spec, feed_index.reshape(-1), axis=0)  44.8 us
    neg x9, other arithmetic, one_term(): lower = jnp.concatenate([-sin_half, cos_half], axis=1)  41 us
    another operation x2, other arithmetic  34.1 us
    dot_general x1, matrix products, beam_power(): jnp.einsum('qe,perfj->prfqj', cosines, real_part, precision=high)  32.8 us
    reshape x2, local copies, waits for them, and re-layouts, body(): spectra = spectra.astype(jnp.bfloat16).reshape(feed_dev, frames, 2, nfreq)  31.3 us
    all_to_all x1, waiting for transfers between devices, all_to_all(jnp.stack(jnp.split(field_in, axis_size('wide'), axis=dimensio...  29.1 us
  transfers between devices with their start and end apart: 2, of which 2 were waited for; matrix products, arithmetic and copies ran while one was open for 3% of the time, Pallas kernels for 0%

profile of v1, /device:TPU:13, one launch (start us, length us, event | category | flops | bytes accessed | tf_op | source)
XLA Modules:
  0.0 760.5 jit_solution(18321137730962282944)
XLA Ops:
  0.0 34.1 %multiply_convert_fusion = (bf16[2048,1024]{1,0:T(8,128)(2,1)S(1)}, bf16[2048,1024]{1,0:T(8,128)(2,1)S(1)}) fusion(), kind=kLoop, calls=%fused_computation.36 | loop fusion | flops 39845888 | bytes 8388608 | tf_op jit(solution)/shard_map/convert.3
  34.1 20.6 %convert_bitcast_fusion = bf16[2048,2048]{0,1:T(8,128)(2,1)} fusion(bf16[2048,2048]{1,0:T(8,128)(2,1)S(1)} %bitcast.158, bf16[2048,1024]{1,0:T(8,128)(2,1)S(1)} %get-tuple-element.129, bf16[2048,1024]{1,0:T(8,128)(2,1)S(1)} %get-tuple-element.130), kind=kOutput, calls=%fused_computation.35 | convolution fusion | flops 17200840704 | bytes 25165824 | tf_op jit(solution)/shard_map/dot_general | solution.py:111
  54.7 12.4 %copy.69 = bf16[2048,2048]{1,0:T(8,128)(2,1)} copy(bf16[2048,2048]{0,1:T(8,128)(2,1)} %convert_bitcast_fusion) | data formatting | bytes 16777216 | tf_op jit(solution)/shard_map/convert_element_type | solution.py:114
  67.1 14.5 %reshape.320 = bf16[128,16,2,1024]{3,2,1,0:T(2,128)(2,1)} reshape(bf16[2048,2048]{1,0:T(8,128)(2,1)} %copy.69) | data formatting | bytes 16777216 | tf_op jit(solution)/shard_map/reshape | solution.py:114
  81.6 16.8 %copy.70 = bf16[128,16,2,1024]{0,1,2,3:T(8,128)(2,1)} copy(bf16[128,16,2,1024]{3,2,1,0:T(2,128)(2,1)} %reshape.320) | data formatting | bytes 16777216 | tf_op jit(solution)/shard_map/reshape | solution.py:114
  98.4 7.1 all-to-all-start
  107.8 179.9 %all-to-all-done = bf16[128,16,2,1024]{0,1,2,3:T(8,128)(2,1)} async-done(((bf16[128,16,2,1024]{0,1,2,3:T(8,128)(2,1)}), bf16[128,16,2,1024]{0,1,2,3:T(8,128)(2,1)}, u32[]{:S(2)}, u32[]{:S(2)}) %all-to-all-start) | async-done | bytes 8388640 | tf_op jit(solution)/shard_map/all_to_all | solution.py:119
  287.7 29.0 %copy.93 = bf16[16,128,16,2,64]{4,2,3,1,0:T(8,128)(2,1)} copy(bf16[16,128,16,2,64]{1,2,3,4,0:T(8,128)(2,1)} %bitcast.5) | data formatting | bytes 16777216 | tf_op jit(solution)/shard_map/all_to_all | solution.py:119
  316.7 25.0 %gather_fusion = bf16[2048,16,2,64]{3,1,2,0:T(8,128)(2,1)} fusion(bf16[2048,16,2,64]{3,1,2,0:T(8,128)(2,1)} %bitcast.150, s32[2048]{0:T(1024)S(1)} %broadcast_clamp_fusion), kind=kCustom, calls=%fused_computation | custom fusion | bytes 16785408 | tf_op jit(solution)/shard_map/jit(_take)/gather | solution.py:51
  341.7 19.8 %copy.94 = bf16[2,4,256,16,2,64]{2,1,0,5,4,3:T(4,128)(2,1)} copy(bf16[2,4,256,16,2,64]{5,3,4,2,1,0:T(8,128)(2,1)} %bitcast.151) | data formatting | bytes 16777216 | tf_op jit(solution)/shard_map/jit(_take)/gather | solution.py:51
  367.3 8.2 %fusion.39 = f32[2,2,4,16,64,256]{5,4,1,3,2,0:T(8,128)} fusion(bf16[2,4,256,16,2,64,1]{2,1,0,5,4,3,6:T(4,128)(2,1)S(1)} %select_bitcast_fusion, f32[256,1,256,2]{2,0,3,1:T(8,128)S(1)} %get-tuple-element.126, f32[256,1,256,2]{2,0,3,1:T(8,128)S(1)} %get-tuple-element.125), kind=kOutput, calls=%fused_computation.49 | convolution fusion | flops 4295753728 | bytes 26214400 | tf_op jit(solution)/shard_map/joni,penrif->poerfj/dot_general | solution.py:53
  375.5 6.5 slice_bitcast_fusion.1
  382.1 18.9 %fusion.31 = f32[2,16,64,256,4]{3,4,2,1,0:T(4,128)} fusion(f32[4,4,1,1,1]{1,0,4,3,2:T(4,128)S(1)} %copy-done.3, f32[2,4,16,64,256]{4,3,2,1,0:T(8,128)S(1)} %get-tuple-element.122), kind=kOutput, calls=%fused_computation.41 | convolution fusion | flops 100663296 | bytes 16777280 | tf_op jit(solution)/shard_map/qe,perfj->prfqj/dot_general | solution.py:64
  401.0 18.4 %fusion.33 = f32[2,16,64,256,4]{3,4,2,1,0:T(4,128)} fusion(f32[4,4,1,1,1]{1,0,4,3,2:T(4,128)S(1)} %copy-done.4, f32[2,4,16,64,256]{4,3,2,1,0:T(8,128)S(1)} %get-tuple-element.122), kind=kOutput, calls=%fused_computation.43 | convolution fusion | flops 100663296 | bytes 16777280 | tf_op jit(solution)/shard_map/qe,perfj->prfqj/dot_general | solution.py:61
  419.4 18.5 %fusion.35 = f32[2,16,64,256,4]{3,4,2,1,0:T(4,128)} fusion(f32[4,4,1,1,1]{1,0,4,3,2:T(4,128)S(1)} %copy-done.4, f32[2,4,16,64,256]{4,3,2,1,0:T(8,128)S(1)} %get-tuple-element.121), kind=kOutput, calls=%fused_computation.45 | convolution fusion | flops 100663296 | bytes 16777280 | tf_op jit(solution)/shard_map/qe,perfj->prfqj/dot_general | solution.py:65
  437.9 32.8 %add_reduce_fusion = f32[16,64,256,4]{2,3,1,0:T(4,128)} fusion(f32[2,16,64,256,4]{3,4,2,1,0:T(4,128)} %fusion.31, f32[2,16,64,256,4]{3,4,2,1,0:T(4,128)} %fusion.35, f32[2,16,64,256,4]{3,4,2,1,0:T(4,128)} %fusion.33, f32[4,4,1,1,1]{1,0,4,3,2:T(4,128)S(1)} %copy-done.3, f32[2,4,16,64,256]{4,3,2,1,0:T(8,128)} %copy-done.1), kind=kOutput, calls=%fused_computation.33 | convolution fusion | flops 116391936 | bytes 37748800 | tf_op jit(solution)/shard_map/qe,perfj->prfqj/dot_general | solution.py:60
  496.4 7.8 %reshape.342 = bf16[16,2,36864]{2,1,0:T(2,128)(2,1)} reshape(bf16[16,9,2,64,64]{4,3,2,1,0:T(8,128)(2,1)} %copy.81) | data formatting | bytes 4718592
  514.9 18.4 %fusion.55 = (f32[1024,1024]{1,0:T(8,128)}, f32[1024,1024]{1,0:T(8,128)}) fusion(s32[1024,1024]{0,1:T(8,128)} %copy.68), kind=kLoop, calls=%fused_computation.65 | loop fusion | flops 13631488 | bytes 12582912 | tf_op jit(solution)/shard_map/sin | solution.py:21
  533.3 29.1 %all-to-all-done.1 = bf16[16,2,36864]{2,1,0:T(2,128)(2,1)S(1)} async-done(((bf16[16,2,36864]{2,1,0:T(2,128)(2,1)}), bf16[16,2,36864]{2,1,0:T(2,128)(2,1)S(1)}, u32[]{:S(2)}, u32[]{:S(2)}) %all-to-all-start.1) | async-done | bytes 2359328 | tf_op jit(solution)/shard_map/all_to_all | solution.py:12
  567.7 6.0 copy.97
  573.7 166.2 %while.15 = (s32[]{:T(128)}, f32[1024,1024]{1,0:T(8,128)}, f32[1024,1024]{1,0:T(8,128)}, f32[9,64,2048]{2,1,0:T(8,128)}, f32[1024,1024]{1,0:T(8,128)}, /*index=5...) while((s32[]{:T(128)}, f32[1024,1024]{1,0:T(8,128)}, ...), condition=%wide.region_3.4_spmd.clone, body=%wide.region_2.3_spmd.clone.sunk | while | flops 584056832 | bytes 64225924 | solution.py:92
  578.8 8.2 %multiply_add_fusion.2 = (f32[1024,1024]{1,0:T(8,128)}, f32[1024,1024]{1,0:T(8,128)}) fusion(f32[1024,1024]{1,0:T(8,128)S(1)} %copy-done, f32[1024,1024]{1,0:T(8,128)} %get-tuple-element.210, f32[1024,1024]{1,0:T(8,128)} %get-tuple-element.199, f32[1024,1024]{1,0:T(8,128)} %get-tuple-element.198, pred[]{:T(512)S(6)} %compare.38), kind=kLoop, calls=%fused_computation.9.clone.1 | loop fusion | flops 8388608 | bytes 25165824 | tf_op jit(solution)/shard_map/while/body/eval_jaxpr/add | solution.py:88
  595.4 10.6 %multiply_add_fusion.2 = (f32[1024,1024]{1,0:T(8,128)}, f32[1024,1024]{1,0:T(8,128)}) fusion(f32[1024,1024]{1,0:T(8,128)S(1)} %copy-done, f32[1024,1024]{1,0:T(8,128)} %get-tuple-element.210, f32[1024,1024]{1,0:T(8,128)} %get-tuple-element.199, f32[1024,1024]{1,0:T(8,128)} %get-tuple-element.198, pred[]{:T(512)S(6)} %compare.38), kind=kLoop, calls=%fused_computation.9.clone.1 | loop fusion | flops 8388608 | bytes 25165824 | tf_op jit(solution)/shard_map/while/body/eval_jaxpr/add | solution.py:88
  614.5 10.6 %multiply_add_fusion.2 = (f32[1024,1024]{1,0:T(8,128)}, f32[1024,1024]{1,0:T(8,128)}) fusion(f32[1024,1024]{1,0:T(8,128)S(1)} %copy-done, f32[1024,1024]{1,0:T(8,128)} %get-tuple-element.210, f32[1024,1024]{1,0:T(8,128)} %get-tuple-element.199, f32[1024,1024]{1,0:T(8,128)} %get-tuple-element.198, pred[]{:T(512)S(6)} %compare.38), kind=kLoop, calls=%fused_computation.9.clone.1 | loop fusion | flops 8388608 | bytes 25165824 | tf_op jit(solution)/shard_map/while/body/eval_jaxpr/add | solution.py:88
  633.7 10.6 %multiply_add_fusion.2 = (f32[1024,1024]{1,0:T(8,128)}, f32[1024,1024]{1,0:T(8,128)}) fusion(f32[1024,1024]{1,0:T(8,128)S(1)} %copy-done, f32[1024,1024]{1,0:T(8,128)} %get-tuple-element.210, f32[1024,1024]{1,0:T(8,128)} %get-tuple-element.199, f32[1024,1024]{1,0:T(8,128)} %get-tuple-element.198, pred[]{:T(512)S(6)} %compare.38), kind=kLoop, calls=%fused_computation.9.clone.1 | loop fusion | flops 8388608 | bytes 25165824 | tf_op jit(solution)/shard_map/while/body/eval_jaxpr/add | solution.py:88
  652.8 10.6 %multiply_add_fusion.2 = (f32[1024,1024]{1,0:T(8,128)}, f32[1024,1024]{1,0:T(8,128)}) fusion(f32[1024,1024]{1,0:T(8,128)S(1)} %copy-done, f32[1024,1024]{1,0:T(8,128)} %get-tuple-element.210, f32[1024,1024]{1,0:T(8,128)} %get-tuple-element.199, f32[1024,1024]{1,0:T(8,128)} %get-tuple-element.198, pred[]{:T(512)S(6)} %compare.38), kind=kLoop, calls=%fused_computation.9.clone.1 | loop fusion | flops 8388608 | bytes 25165824 | tf_op jit(solution)/shard_map/while/body/eval_jaxpr/add | solution.py:88
  671.9 10.6 %multiply_add_fusion.2 = (f32[1024,1024]{1,0:T(8,128)}, f32[1024,1024]{1,0:T(8,128)}) fusion(f32[1024,1024]{1,0:T(8,128)S(1)} %copy-done, f32[1024,1024]{1,0:T(8,128)} %get-tuple-element.210, f32[1024,1024]{1,0:T(8,128)} %get-tuple-element.199, f32[1024,1024]{1,0:T(8,128)} %get-tuple-element.198, pred[]{:T(512)S(6)} %compare.38), kind=kLoop, calls=%fused_computation.9.clone.1 | loop fusion | flops 8388608 | bytes 25165824 | tf_op jit(solution)/shard_map/while/body/eval_jaxpr/add | solution.py:88
  691.0 10.6 %multiply_add_fusion.2 = (f32[1024,1024]{1,0:T(8,128)}, f32[1024,1024]{1,0:T(8,128)}) fusion(f32[1024,1024]{1,0:T(8,128)S(1)} %copy-done, f32[1024,1024]{1,0:T(8,128)} %get-tuple-element.210, f32[1024,1024]{1,0:T(8,128)} %get-tuple-element.199, f32[1024,1024]{1,0:T(8,128)} %get-tuple-element.198, pred[]{:T(512)S(6)} %compare.38), kind=kLoop, calls=%fused_computation.9.clone.1 | loop fusion | flops 8388608 | bytes 25165824 | tf_op jit(solution)/shard_map/while/body/eval_jaxpr/add | solution.py:88
  710.2 10.6 %multiply_add_fusion.2 = (f32[1024,1024]{1,0:T(8,128)}, f32[1024,1024]{1,0:T(8,128)}) fusion(f32[1024,1024]{1,0:T(8,128)S(1)} %copy-done, f32[1024,1024]{1,0:T(8,128)} %get-tuple-element.210, f32[1024,1024]{1,0:T(8,128)} %get-tuple-element.199, f32[1024,1024]{1,0:T(8,128)} %get-tuple-element.198, pred[]{:T(512)S(6)} %compare.38), kind=kLoop, calls=%fused_computation.9.clone.1 | loop fusion | flops 8388608 | bytes 25165824 | tf_op jit(solution)/shard_map/while/body/eval_jaxpr/add | solution.py:88
  729.3 10.6 %multiply_add_fusion.2 = (f32[1024,1024]{1,0:T(8,128)}, f32[1024,1024]{1,0:T(8,128)}) fusion(f32[1024,1024]{1,0:T(8,128)S(1)} %copy-done, f32[1024,1024]{1,0:T(8,128)} %get-tuple-element.210, f32[1024,1024]{1,0:T(8,128)} %get-tuple-element.199, f32[1024,1024]{1,0:T(8,128)} %get-tuple-element.198, pred[]{:T(512)S(6)} %compare.38), kind=kLoop, calls=%fused_computation.9.clone.1 | loop fusion | flops 8388608 | bytes 25165824 | tf_op jit(solution)/shard_map/while/body/eval_jaxpr/add | solution.py:88
  739.9 7.4 reshape.323
  747.3 13.0 %fusion.48 = f32[64,16,1024]{2,1,0:T(8,128)} fusion(f32[9,64,2,1024]{3,2,1,0:T(2,128)} %reshape.323, f32[16,1,9]{2,0,1:T(8,128)S(1)} %get-tuple-element.128, f32[16,1,9]{2,0,1:T(8,128)S(1)} %get-tuple-element.127), kind=kOutput, calls=%fused_computation.60 | convolution fusion | flops 226492704 | bytes 8914048 | tf_op jit(solution)/shard_map/tuk,kbud->btd/dot_general | solution.py:104
  (100 shorter events, 122.2 us)
Async XLA Ops:
  0.0 34.1 %copy-start.6 = (bf16[128,16,2048]{2,1,0:T(8,128)(2,1)S(1)}, bf16[128,16,2048]{2,1,0:T(8,128)(2,1)}, u32[]{:S(2)}) copy-start(bf16[128,16,2048]{2,1,0:T(8,128)(2,1)} %param.7) | copy-start | bytes 25165828
  98.4 7.1 copy-start.5
  98.4 189.3 %all-to-all-start = ((bf16[128,16,2,1024]{0,1,2,3:T(8,128)(2,1)}), bf16[128,16,2,1024]{0,1,2,3:T(8,128)(2,1)}, u32[]{:S(2)}, u32[]{:S(2)}) async-start(bf16[128,16,2,1024]{0,1,2,3:T(8,128)(2,1)} %copy.70), calls=%async_computation | async-start | bytes 16777216 | tf_op jit(solution)/shard_map/all_to_all | solution.py:119
  375.5 6.5 copy-start.3
  382.0 37.4 %copy-start.1 = (f32[2,4,16,64,256]{4,3,2,1,0:T(8,128)}, f32[2,4,16,64,256]{4,3,2,1,0:T(8,128)S(1)}, u32[]{:S(2)}) copy-start(f32[2,4,16,64,256]{4,3,2,1,0:T(8,128)S(1)} %get-tuple-element.121) | copy-start | bytes 25165828
  382.0 18.9 %copy-start.4 = (f32[4,4,1,1,1]{1,0,4,3,2:T(4,128)S(1)}, f32[4,4,1,1,1]{1,0,4,3,2:T(4,128)}, u32[]{:S(2)}) copy-start(f32[4,4,1,1,1]{1,0,4,3,2:T(4,128)} %constant.123) | copy-start | bytes 196
  470.7 5.4 copy-start.2
  504.2 58.2 %all-to-all-start.1 = ((bf16[16,2,36864]{2,1,0:T(2,128)(2,1)}), bf16[16,2,36864]{2,1,0:T(2,128)(2,1)S(1)}, u32[]{:S(2)}, u32[]{:S(2)}) async-start(bf16[16,2,36864]{2,1,0:T(2,128)(2,1)} %reshape.342), calls=%async_computation.1 | async-start | bytes 4718592 | tf_op jit(solution)/shard_map/all_to_all | solution.py:12
  576.3 2.4 copy-start
  593.0 2.5 copy-start
  612.1 2.4 copy-start
  631.2 2.4 copy-start
  650.3 2.4 copy-start
  669.4 2.4 copy-start
  688.5 2.5 copy-start
  707.7 2.5 copy-start
  726.8 2.5 copy-start
